TPU v7x, 32 devices: a whole 2x2x4 slice. The times are simulated.
32 devices in a mesh: row: 4 (over y, x), col: 8 (over z, core).
Axes of the slice: x: 2, y: 2, z: 4, core: 2. Of those that a mesh axis runs over, the one named last changes fastest.
Arguments:
- out_grad: bfloat16 [4096, 8192], P('row', 'col'), may hold values from -0.059814453 to 0.059814453
- hidden: bfloat16 [4096, 28672], P('row', 'col'), may hold values from -6 to 6
- basis: bfloat16 [8192, 1024], P('col'), may hold values from -0.0625 to 0.0625
- weight: bfloat16 [8192, 28672], P('row', 'col'), may hold values from -6 to 6
- first_moment: float32 [1024, 28672], P('row', 'col'), may hold values from -4 to 4
- second_moment: float32 [1024, 28672], P('row', 'col'), may hold values from 0.25 to 4
Outputs:
- new_weight: bfloat16 [8192, 28672], P('row', 'col')
- new_first: float32 [1024, 28672], P('row', 'col')
- new_second: float32 [1024, 28672], P('row', 'col')
All inputs are finite; a program needn't handle non-finite values.
Results may differ from a plain program's by a relative error of at most 0.0039.
Values may be sent and summed in bfloat16 or wider, within the bound.
A program may use at most 128 MiB of HBM per device.

v0:
```python
import jax
import jax.numpy as jnp
from jax import lax
from jax.sharding import PartitionSpec as P

STEP_COUNT = 1000


beta_one = 0.9
beta_two = 0.999
epsilon = 1e-08
step_size = 1.0


def spread(block, axis, source):
    block = jnp.where(lax.axis_index(axis) == source, block, jnp.zeros_like(block))
    return lax.psum(block, axis)


def local(out_grad, hidden, basis, weight, first_moment, second_moment):
    partial_value = jnp.dot(out_grad, basis, preferred_element_type=jnp.float32)
    projected = lax.psum(partial_value, "col").astype(jnp.bfloat16)
    columns = projected
    gradient = lax.psum_scatter(
        lax.dot_general(
            columns, hidden, (((0,), (0,)), ((), ())), preferred_element_type=jnp.float32
        ).astype(jnp.bfloat16),
        "row",
        scatter_dimension=0,
        tiled=True,
    ).astype(jnp.float32)
    new_first = beta_one * first_moment + (1.0 - beta_one) * gradient
    new_second = beta_two * second_moment + (1.0 - beta_two) * gradient * gradient
    first_hat = new_first / (1.0 - beta_one**STEP_COUNT)
    second_hat = new_second / (1.0 - beta_two**STEP_COUNT)
    direction = (first_hat / (jnp.sqrt(second_hat) + epsilon)).astype(jnp.bfloat16)
    per_band = lax.axis_size("col") // lax.axis_size("row")
    blocks = [
        spread(basis, "col", lax.axis_index("row") * per_band + offset)
        for offset in range(per_band)
    ]
    local_basis = jnp.concatenate(blocks, 0)
    initial = jnp.zeros((local_basis.shape[0], direction.shape[1]), jnp.float32)
    portion = lax.all_gather(direction, "row", axis=0, tiled=True)
    columns = lax.slice_in_dim(local_basis, 0, portion.shape[0], axis=1)
    update = initial + jnp.dot(columns, portion, preferred_element_type=jnp.float32)
    new_weight = (weight.astype(jnp.float32) - step_size * update).astype(jnp.bfloat16)
    return (new_weight, new_first, new_second)


def solution(mesh):
    in_specs = (
        P("row", "col"),
        P("row", "col"),
        P("col", None),
        P("row", "col"),
        P("row", "col"),
        P("row", "col"),
    )
    out_specs = (P("row", "col"), P("row", "col"), P("row", "col"))
    return jax.shard_map(local, mesh=mesh, in_specs=in_specs, out_specs=out_specs, check_vma=False)
```

profile of v0, /device:TPU:25, one launch (start us, length us, event | category | flops | bytes accessed | tf_op | source)
XLA Modules:
  0.0 315.0 jit_solution(15711441214757857168)
XLA Ops:
  8.0 0.0 copy-start
  8.0 0.0 reduce-scatter.2.cloned.1.call-start
  8.1 1.5 copy-done
  9.6 5.9 %fusion.9 = f32[1024,1024]{1,0:T(8,128)} fusion(bf16[1024,1024]{1,0:T(8,128)(2,1)S(1)} %copy-done, bf16[1024,1024]{1,0:T(8,128)(2,1)} %param.8), kind=kOutput, calls=%fused_computation.14 | convolution fusion | flops 2147483648 | bytes 8388608 | tf_op jit(solution)/shard_map/dot_general | solution.py:21
  15.5 86.6 %all-reduce.5 = bf16[1024,1024]{1,0:T(8,128)(2,1)S(1)} all-reduce(f32[1024,1024]{1,0:T(8,128)} %fusion.9), channel_id=1, replica_groups=mesh['row'=4,'col'=8] {'col'}, use_global_device_ids=true, to_apply=%region_2.3 | all-reduce | flops 1048576 | bytes 6291456 | tf_op jit(solution)/shard_map/psum | solution.py:22
  102.1 13.0 %convolution_convert_fusion = bf16[1024,3584]{1,0:T(8,128)(2,1)} fusion(bf16[1024,3584]{1,0:T(8,128)(2,1)} %param.7, bf16[1024,1024]{1,0:T(8,128)(2,1)S(1)} %all-reduce.5), kind=kOutput, calls=%fused_computation.1 | convolution fusion | flops 7519862784 | bytes 16777216 | tf_op jit(solution)/shard_map/dot_general | solution.py:25
  115.1 0.0 copy-start.2
  115.1 0.0 reduce-scatter.2.cloned.1.call-update
  115.2 0.0 all-reduce.4.cloned.1.call-start
  115.2 1.5 copy-done.2
  116.7 2.3 broadcast_select_fusion.1
  119.0 0.0 all-reduce.4.cloned.1.call-update
  119.1 0.2 all-gather.2.cloned.1.call-start
  119.3 76.3 %reduce-scatter.2.cloned.1.call-done = bf16[256,3584]{1,0:T(8,128)(2,1)} async-done(((bf16[1024,3584]{1,0:T(8,128)(2,1)}), bf16[256,3584]{1,0:T(8,128)(2,1)}) %reduce-scatter.2.cloned.1.call-update) | async-done | bytes 1835024 | tf_op jit(solution)/shard_map/reduce_scatter | solution.py:24
  195.6 8.8 %divide_convert_fusion = (bf16[256,3584]{1,0:T(8,128)(2,1)}, f32[256,3584]{1,0:T(8,128)}, f32[256,3584]{1,0:T(8,128)}) fusion(bf16[256,3584]{1,0:T(8,128)(2,1)} %reduce-scatter.2.cloned.1.call-done, f32[256,3584]{1,0:T(8,128)} %param.11, f32[256,3584]{1,0:T(8,128)} %param.10), kind=kLoop, calls=%fused_computation.9 | loop fusion | flops 11010048 | bytes 18350080 | tf_op jit(solution)/shard_map/convert_element_type | solution.py:36
  204.4 0.0 all-gather.2.cloned.1.call-update
  204.5 11.8 %all-reduce.4.cloned.1.call-done = (bf16[1024,1024]{1,0:T(8,128)(2,1)}, bf16[1024,1024]{1,0:T(8,128)(2,1)}) async-done(((bf16[1024,1024]{1,0:T(8,128)(2,1)}, bf16[1024,1024]{1,0:T(8,128)(2,1)}), (bf16[1024,1024]{1,0:T(8,128)(2,1)}, bf16[1024,1024]{1,0:T(8,128)(2,1)})) %all-reduce.4.cloned.1.call-update) | async-done | bytes 4194320 | tf_op jit(solution)/shard_map/psum | solution.py:17
  216.2 67.1 %all-gather.2.cloned.1.call-done = bf16[1024,3584]{1,0:T(8,128)(2,1)} async-done(((bf16[256,3584]{1,0:T(8,128)(2,1)}), bf16[1024,3584]{1,0:T(8,128)(2,1)}) %all-gather.2.cloned.1.call-update) | async-done | bytes 7340048 | tf_op jit(solution)/shard_map/all_gather | solution.py:44
  283.4 0.0 copy-start.1
  283.4 24.2 %subtract_convert_fusion = bf16[2048,3584]{1,0:T(8,128)(2,1)} fusion(bf16[2048,3584]{1,0:T(8,128)(2,1)} %param.9, bf16[1024,3584]{1,0:T(8,128)(2,1)} %all-gather.2.cloned.1.call-done, bf16[1024,1024]{1,0:T(8,128)(2,1)} %get-tuple-element.3, bf16[1024,1024]{1,0:T(8,128)(2,1)} %get-tuple-element.4), kind=kOutput, calls=%fused_computation | convolution fusion | flops 15062794240 | bytes 40894464 | tf_op jit(solution)/shard_map/dot_general | solution.py:46
  307.6 0.0 copy-done.1
Async XLA Ops:
  8.0 1.6 copy-start
  8.0 187.6 %reduce-scatter.2.cloned.1.call-start = ((), (), s32[]{:S(2)}) async-start(), calls=%async_computation.1 | async-start | bytes 9175040 | tf_op jit(solution)/shard_map/reduce_scatter | solution.py:24
  115.1 1.6 copy-start.2
  115.2 101.1 %all-reduce.4.cloned.1.call-start = ((), (), s32[]{:S(2)}) async-start(), calls=%async_computation.3 | async-start | bytes 8388608 | tf_op jit(solution)/shard_map/psum | solution.py:17
  119.1 164.3 %all-gather.2.cloned.1.call-start = ((), (), s32[]{:S(2)}) async-start(), calls=%async_computation.2 | async-start | bytes 9175040 | tf_op jit(solution)/shard_map/all_gather | solution.py:44
  283.4 24.2 %copy-start.1 = (bf16[1024,1024]{1,0:T(8,128)(2,1)S(1)}, bf16[1024,1024]{1,0:T(8,128)(2,1)}, u32[]{:S(2)}) copy-start(bf16[1024,1024]{1,0:T(8,128)(2,1)} %param.6) | copy-start | bytes 6291460
Sparse Core Ops, SparseCore 0:
  115.3 80.2 reduce-scatter.1
  204.6 78.7 all-gather.1
Sparse Core Ops, SparseCore 1:
  119.1 97.0 all-reduce.3
where the time goes:
time: 317 us; the launch traced here: 315 us
  waiting for transfers between devices  155 us (49%)
  blocking collectives  86.6 us (27%)
  matrix products  43.1 us (14%)
  between operations  15.5 us (5%)
  other arithmetic  11.1 us (4%)
    psum x1, blocking collectives, local(): projected = lax.psum(partial_value, 'col').astype(jnp.bfloat16)  86.6 us
    reduce_scatter x1, waiting for transfers between devices, local(): lax.psum_scatter(lax.dot_general(columns, hidden, (((0,), (0,)), ((), ())...  76.3 us
    all_gather x1, waiting for transfers between devices, local(): portion = lax.all_gather(direction, 'row', axis=0, tiled=True)  67.1 us
    dot_general x1, matrix products, local(): jnp.dot(columns, portion, preferred_element_type=jnp.float32)  24.2 us
    dot_general x1, matrix products, local(): lax.dot_general(columns, hidden, (((0,), (0,)), ((), ())), preferred_elem...  13 us
    psum x1, waiting for transfers between devices, spread(): return lax.psum(block, axis)  11.8 us
    convert_element_type x1, other arithmetic, local(): (first_hat / (jnp.sqrt(second_hat) + epsilon)).astype(jnp.bfloat16)  8.84 us
  transfers between devices with their start and end apart: 3, of which 3 were waited for; matrix products, arithmetic and copies ran while one was open for 4% of the time, Pallas kernels for 0%

commit v1 on v0

v1 whole, which is shorter than its diff:
```python
import functools

import jax
import jax.numpy as jnp
from jax import lax
from jax.experimental import pallas as pl
from jax.experimental.pallas import tpu as pltpu
from jax.sharding import PartitionSpec as P

STEP_COUNT = 1000


beta_one = 0.9
beta_two = 0.999
epsilon = 1e-08
step_size = 1.0

MESH = pl.DeviceIdType.MESH


def row_kernel(
    A, B, steps, rb, W,
    proj, hidden, first, second,
    gathered, new_first, new_second,
    hid, par, one_b, one_a, mid_b, mid_a, two_b, two_a, gat, mom_one, mom_two,
    load, out_sem,
    s1b, r1b, s1a, r1a, s2b, r2b, s2a, r2a,
    sgb, rgb, sga, rga, srb, rrb, sra, rra,
):
    row = lax.axis_index("row")
    a, b = row // B, lax.rem(row, B)

    def to_a(k):
        return {"row": lax.rem(a + k, A) * B + b}

    def to_b(k):
        return {"row": a * B + lax.rem(b + k, B)}

    def span(s):
        return pl.ds(pl.multiple_of(s * 2 * W, 2 * W), 2 * W)

    def loads(s):
        return (
            pltpu.make_async_copy(hidden.at[:, span(s)], hid.at[s], load.at[0, s]),
            pltpu.make_async_copy(first.at[:, span(s)], mom_one.at[s], load.at[1, s]),
            pltpu.make_async_copy(second.at[:, span(s)], mom_two.at[s], load.at[2, s]),
        )

    def stores(s):
        return (
            pltpu.make_async_copy(mom_one.at[s], new_first.at[:, span(s)], out_sem.at[1, s]),
            pltpu.make_async_copy(mom_two.at[s], new_second.at[:, span(s)], out_sem.at[2, s]),
        )

    def remote(src, dst, send, recv, device):
        return pltpu.make_async_remote_copy(
            src_ref=src, dst_ref=dst, send_sem=send, recv_sem=recv,
            device_id=device, device_id_type=MESH,
        )

    def first_hops(s):
        for k in range(1, B):
            yield remote(par.at[s, 0, :, lax.rem(b + k, B)], one_b.at[s, k - 1],
                         s1b.at[s, k - 1], r1b.at[s, k - 1], to_b(k))
        for k in range(1, A):
            yield remote(par.at[s, 1, lax.rem(a + k, A)], one_a.at[s, k - 1],
                         s1a.at[s, k - 1], r1a.at[s, k - 1], to_a(k))

    def second_hops(s):
        for k in range(1, A):
            yield remote(mid_b.at[s, lax.rem(a + k, A)], two_b.at[s, k - 1],
                         s2b.at[s, k - 1], r2b.at[s, k - 1], to_a(k))
        for k in range(1, B):
            yield remote(mid_a.at[s, lax.rem(b + k, B)], two_a.at[s, k - 1],
                         s2a.at[s, k - 1], r2a.at[s, k - 1], to_b(k))

    def own_sends(s):
        for k in range(1, B):
            yield remote(gat.at[s, :, a, b], gat.at[s, :, a, b],
                         sgb.at[s, k - 1], rgb.at[s, k - 1], to_b(k))
        for k in range(1, A):
            yield remote(gat.at[s, :, a, b], gat.at[s, :, a, b],
                         sga.at[s, k - 1], rga.at[s, k - 1], to_a(k))

    def relays(s):
        for j in range(1, B):
            for k in range(1, A):
                block = gat.at[s, 0, a, lax.rem(b + j, B)]
                i = (j - 1) * (A - 1) + k - 1
                yield remote(block, block, srb.at[s, i], rrb.at[s, i], to_a(k))
        for j in range(1, A):
            for k in range(1, B):
                block = gat.at[s, 1, lax.rem(a + j, A), b]
                i = (j - 1) * (B - 1) + k - 1
                yield remote(block, block, sra.at[s, i], rra.at[s, i], to_b(k))

    def result(s):
        return pltpu.make_async_copy(gat.at[s], gathered.at[s], out_sem.at[0, s])

    def every(body):
        lax.fori_loop(0, steps, lambda s, c: (body(s), c)[1], 0)

    every(lambda s: [c.start() for c in loads(s)])

    barrier = pltpu.get_barrier_semaphore()
    for k in range(1, B):
        pl.semaphore_signal(barrier, inc=1, device_id=to_b(k), device_id_type=MESH)
    for k in range(1, A):
        pl.semaphore_signal(barrier, inc=1, device_id=to_a(k), device_id_type=MESH)
    pl.semaphore_wait(barrier, A + B - 2)

    f32 = jnp.float32

    def turn(it, carry):
        @pl.when(it < steps)
        def _():
            s = it
            loads(s)[0].wait()
            for t in range(2):
                got = jnp.dot(proj[...], hid[s, :, t * W:(t + 1) * W],
                              preferred_element_type=f32)
                par[s, t] = got.astype(jnp.bfloat16).reshape(A, B, rb, W)
            for c in first_hops(s):
                c.start()

        @pl.when((it >= 1) & (it < steps + 1))
        def _():
            s = it - 1
            for c in first_hops(s):
                c.wait_recv()
            for i in range(A):
                total = par[s, 0, i, b].astype(f32)
                for k in range(B - 1):
                    total += one_b[s, k, i].astype(f32)
                mid_b[s, i] = total.astype(jnp.bfloat16)
            for i in range(B):
                total = par[s, 1, a, i].astype(f32)
                for k in range(A - 1):
                    total += one_a[s, k, i].astype(f32)
                mid_a[s, i] = total.astype(jnp.bfloat16)
            for c in second_hops(s):
                c.start()

        @pl.when((it >= 2) & (it < steps + 2))
        def _():
            s = it - 2
            for c in second_hops(s):
                c.wait_recv()
            for c in loads(s)[1:]:
                c.wait()
            for t in range(2):
                if t == 0:
                    gradient = mid_b[s, a].astype(f32)
                    for k in range(A - 1):
                        gradient += two_b[s, k].astype(f32)
                else:
                    gradient = mid_a[s, b].astype(f32)
                    for k in range(B - 1):
                        gradient += two_a[s, k].astype(f32)
                cols = slice(t * W, (t + 1) * W)
                one = beta_one * mom_one[s, :, cols] + (1.0 - beta_one) * gradient
                two = beta_two * mom_two[s, :, cols] + (1.0 - beta_two) * gradient * gradient
                first_hat = one / (1.0 - beta_one**STEP_COUNT)
                second_hat = two / (1.0 - beta_two**STEP_COUNT)
                gat[s, t, a, b] = (first_hat / (jnp.sqrt(second_hat) + epsilon)).astype(jnp.bfloat16)
                mom_one[s, :, cols] = one
                mom_two[s, :, cols] = two
            for c in own_sends(s):
                c.start()
            for c in stores(s):
                c.start()

        @pl.when((it >= 3) & (it < steps + 3))
        def _():
            s = it - 3
            for c in own_sends(s):
                c.wait_recv()
            for c in relays(s):
                c.start()

        @pl.when(it >= 4)
        def _():
            s = it - 4
            for c in relays(s):
                c.wait_recv()
            result(s).start()

        return carry

    lax.fori_loop(0, steps + 4, turn, 0)

    def finish(s):
        for group in (first_hops, second_hops, own_sends, relays):
            for c in group(s):
                c.wait_send()
        for c in stores(s):
            c.wait()
        result(s).wait()

    every(finish)


def row_part(rows, proj, hidden, first, second):
    B = 2 if rows % 2 == 0 else 1
    A = rows // B
    rank, tokens = proj.shape
    rb, cols = first.shape
    W = 256 if cols % 512 == 0 else 128
    steps = cols // (2 * W)
    bf16, f32 = jnp.bfloat16, jnp.float32
    nb, na = max(B - 1, 1), max(A - 1, 1)
    nr = na * nb

    def pair(n):
        return [pltpu.SemaphoreType.DMA((steps, n)), pltpu.SemaphoreType.DMA((steps, n))]

    anywhere = pl.BlockSpec(memory_space=pl.ANY)
    return pl.pallas_call(
        functools.partial(row_kernel, A, B, steps, rb, W),
        name="row_part",
        out_shape=(
            jax.ShapeDtypeStruct((steps, 2, A, B, rb, W), bf16),
            jax.ShapeDtypeStruct(first.shape, f32),
            jax.ShapeDtypeStruct(second.shape, f32),
        ),
        in_specs=[pl.BlockSpec(memory_space=pltpu.VMEM), anywhere, anywhere, anywhere],
        out_specs=(anywhere, anywhere, anywhere),
        scratch_shapes=[
            pltpu.VMEM((steps, tokens, 2 * W), bf16),
            pltpu.VMEM((steps, 2, A, B, rb, W), bf16),
            pltpu.VMEM((steps, nb, A, rb, W), bf16),
            pltpu.VMEM((steps, na, B, rb, W), bf16),
            pltpu.VMEM((steps, A, rb, W), bf16),
            pltpu.VMEM((steps, B, rb, W), bf16),
            pltpu.VMEM((steps, na, rb, W), bf16),
            pltpu.VMEM((steps, nb, rb, W), bf16),
            pltpu.VMEM((steps, 2, A, B, rb, W), bf16),
            pltpu.VMEM((steps, rb, 2 * W), f32),
            pltpu.VMEM((steps, rb, 2 * W), f32),
            pltpu.SemaphoreType.DMA((3, steps)),
            pltpu.SemaphoreType.DMA((3, steps)),
        ] + pair(nb) + pair(na) + pair(na) + pair(nb) + pair(nb) + pair(na) + pair(nr) + pair(nr),
        compiler_params=pltpu.CompilerParams(
            collective_id=0, has_side_effects=True, vmem_limit_bytes=60 << 20
        ),
        cost_estimate=pl.CostEstimate(
            flops=2 * rank * tokens * cols * 8, bytes_accessed=400 << 20, transcendentals=0
        ),
    )(proj, hidden, first, second)


def update_kernel(W, which, basis, direction, weight, out):
    for t in range(2):
        cols = slice(t * W, (t + 1) * W)
        update = jnp.dot(basis[...], direction[0, t], preferred_element_type=jnp.float32)
        out[:, cols] = (weight[:, cols].astype(jnp.float32) - step_size * update).astype(jnp.bfloat16)


def apply_update(index, basis, gathered, weight):
    steps, _, rank, W = gathered.shape
    rows, cols = weight.shape
    wide = pl.BlockSpec((rows, 2 * W), lambda j, r: (0, j))
    return pl.pallas_call(
        functools.partial(update_kernel, W),
        name="apply_update",
        out_shape=jax.ShapeDtypeStruct(weight.shape, weight.dtype),
        grid_spec=pltpu.PrefetchScalarGridSpec(
            num_scalar_prefetch=1,
            grid=(steps,),
            in_specs=[
                pl.BlockSpec((rows, rank), lambda j, r: (r[0], 0), pipeline_mode=pl.Buffered(1)),
                pl.BlockSpec((1, 2, rank, W), lambda j, r: (j, 0, 0, 0)),
                wide,
            ],
            out_specs=wide,
        ),
        compiler_params=pltpu.CompilerParams(
            dimension_semantics=("arbitrary",), vmem_limit_bytes=56 << 20
        ),
        cost_estimate=pl.CostEstimate(
            flops=2 * rank * rows * cols, bytes_accessed=3 * weight.size * 2, transcendentals=0
        ),
    )(index, basis, gathered, weight)


def local(rows, out_grad, hidden, basis, weight, first_moment, second_moment):
    part = lax.dot_general(
        basis, out_grad, (((0,), (1,)), ((), ())), preferred_element_type=jnp.float32
    ).astype(jnp.bfloat16)
    proj = lax.psum_scatter(part, "col", scatter_dimension=0, tiled=True)
    proj = lax.all_gather(proj, "col", axis=0, tiled=True)
    late, proj = lax.optimization_barrier((basis, proj))
    whole = lax.all_gather(late, "col", axis=0, tiled=True)
    gathered, new_first, new_second = row_part(rows, proj, hidden, first_moment, second_moment)
    steps, W = gathered.shape[0], gathered.shape[-1]
    gathered = gathered.reshape(steps, 2, -1, W)
    index = lax.axis_index("row").astype(jnp.int32).reshape(1)
    new_weight = apply_update(index, whole, gathered, weight)
    return (new_weight, new_first, new_second)


def solution(mesh):
    in_specs = (
        P("row", "col"),
        P("row", "col"),
        P("col", None),
        P("row", "col"),
        P("row", "col"),
        P("row", "col"),
    )
    out_specs = (P("row", "col"), P("row", "col"), P("row", "col"))
    return jax.shard_map(
        functools.partial(local, mesh.shape["row"]),
        mesh=mesh, in_specs=in_specs, out_specs=out_specs, check_vma=False,
    )
```

time: 317 us -> 268 us (0.85)
  Pallas kernels: 0 us -> 148 us
  blocking collectives: 86.6 us -> 0 us
  waiting for transfers between devices: 155 us -> 89.4 us
  matrix products: 43.1 us -> 5.29 us
  other arithmetic: 11.1 us -> 0 us
  local copies, waits for them, and re-layouts: 3.06 us -> 6.74 us
    pallas_call x0 -> x2, Pallas kernels: none -> 148 us  [the longest x1 126 us: row_part(): pl.pallas_call(functools.partial(row_kernel, A, B, steps, rb, W), name='r...]
    psum x1 -> x0, blocking collectives: 86.6 us -> none  [local(): projected = lax.psum(partial_value, 'col').astype(jnp.bfloat16)]
    reduce_scatter x1, waiting for transfers between devices: 76.3 us -> 35.5 us  [local(): proj = lax.psum_scatter(part, 'col', scatter_dimension=0, tiled=True)]
    dot_general x3 -> x1, matrix products: 43.1 us -> 5.29 us  [local(): lax.dot_general(basis, out_grad, (((0,), (1,)), ((), ())), preferred_elem...]
    all_gather x1 -> x2, waiting for transfers between devices: 67.1 us -> 53.9 us  [the longest x1 29.6 us: local(): proj = lax.all_gather(proj, 'col', axis=0, tiled=True)]
    psum x1 -> x0, waiting for transfers between devices: 11.8 us -> none  [spread(): return lax.psum(block, axis)]
    convert_element_type x1 -> x0, other arithmetic: 8.84 us -> none  [local(): (first_hat / (jnp.sqrt(second_hat) + epsilon)).astype(jnp.bfloat16)]
    unnamed x6 -> x10, local copies, waits for them, and re-layouts: 3.06 us -> 6.74 us
  transfers between devices with their start and end apart: 3 -> 3, of which waited for: 3 -> 3; matrix products, arithmetic and copies ran while one was open for 4% -> 0% of each run, Pallas kernels for 0% -> 48%
where the time goes in v1:
time: 268 us; the launch traced here: 264 us
  Pallas kernels  148 us (55%)
  waiting for transfers between devices  89.4 us (33%)
  between operations  13.8 us (5%)
  local copies, waits for them, and re-layouts  6.74 us (3%)
  matrix products  5.29 us (2%)
    pallas_call x1, Pallas kernels, row_part(): pl.pallas_call(functools.partial(row_kernel, A, B, steps, rb, W), name='r...  126 us
    reduce_scatter x1, waiting for transfers between devices, local(): proj = lax.psum_scatter(part, 'col', scatter_dimension=0, tiled=True)  35.5 us
    all_gather x1, waiting for transfers between devices, local(): proj = lax.all_gather(proj, 'col', axis=0, tiled=True)  29.6 us
    all_gather x1, waiting for transfers between devices, local(): whole = lax.all_gather(late, 'col', axis=0, tiled=True)  24.3 us
    pallas_call x1, Pallas kernels, apply_update(): pl.pallas_call(functools.partial(update_kernel, W), name='apply_update',...  22.1 us
    unnamed x10, local copies, waits for them, and re-layouts  6.74 us
  transfers between devices with their start and end apart: 3, of which 3 were waited for; matrix products, arithmetic and copies ran while one was open for 0% of the time, Pallas kernels for 48%

profile of v1, /device:TPU:25, one launch (start us, length us, event | category | flops | bytes accessed | tf_op | source)
XLA Modules:
  0.0 263.7 jit_solution(54521654120413259)
XLA Ops:
  7.2 0.0 copy-start
  7.2 0.0 reduce-scatter.2.cloned.1.call-start
  7.2 1.5 copy-done
  8.8 5.3 %convolution_convert_fusion = bf16[1024,1024]{1,0:T(8,128)(2,1)} fusion(bf16[1024,1024]{1,0:T(8,128)(2,1)} %param.8, bf16[1024,1024]{1,0:T(8,128)(2,1)S(1)} %copy-done), kind=kOutput, calls=%fused_computation | convolution fusion | flops 2148532224 | bytes 6291456 | tf_op jit(solution)/shard_map/dot_general | solution.py:287
  14.1 0.0 reduce-scatter.2.cloned.1.call-update
  14.1 0.0 all-gather.3.cloned.1.call-start
  14.1 35.5 %reduce-scatter.2.cloned.1.call-done = bf16[128,1024]{1,0:T(8,128)(2,1)} async-done(((bf16[1024,1024]{1,0:T(8,128)(2,1)}), bf16[128,1024]{1,0:T(8,128)(2,1)}) %reduce-scatter.2.cloned.1.call-update) | async-done | bytes 262160 | tf_op jit(solution)/shard_map/reduce_scatter | solution.py:290
  49.6 0.0 all-gather.3.cloned.1.call-update
  49.6 0.0 all-gather.5.cloned.1.call-start
  49.7 29.6 %all-gather.3.cloned.1.call-done.proj = bf16[1024,1024]{1,0:T(8,128)(2,1)} async-done(((bf16[128,1024]{1,0:T(8,128)(2,1)}), bf16[1024,1024]{1,0:T(8,128)(2,1)}) %all-gather.3.cloned.1.call-update) | async-done | bytes 2097168 | tf_op jit(solution)/shard_map/all_gather | solution.py:291
  79.3 0.0 all-gather.5.cloned.1.call-update
  79.3 126.2 %row_part.1 = (bf16[7,2,2,2,256,256]{5,4,3,2,1,0:T(8,128)(2,1)}, f32[256,3584]{1,0:T(8,128)}, f32[256,3584]{1,0:T(8,128)}) custom-call(bf16[1024,1024]{1,0:T(8,128)(2,1)} %all-gather.3.cloned.1.call-done.proj, bf16[1024,3584]{1,0:T(8,128)(2,1)} %hidden.1, f32[256,3584]{1,0:T(8,128)} %first.1, f32[256,3584]{1,0:T(8,128)} %second.1), custom_call_target="tpu_custom_call" | custom-call | flops 60129542144 | bytes 419430400 | tf_op jit(solution)/shard_map/row_part/pallas_call | solution.py:218
  205.5 24.3 %all-gather.5.cloned.1.call-done.basis = bf16[8192,1024]{1,0:T(8,128)(2,1)} async-done(((bf16[1024,1024]{1,0:T(8,128)(2,1)}), bf16[8192,1024]{1,0:T(8,128)(2,1)}) %all-gather.5.cloned.1.call-update) | async-done | bytes 16777232 | tf_op jit(solution)/shard_map/all_gather | solution.py:293
  229.9 0.0 copy-start.3
  229.9 22.1 %apply_update.1 = bf16[2048,3584]{1,0:T(8,128)(2,1)} custom-call(s32[1]{0:T(128)} %bitcast.which, bf16[8192,1024]{1,0:T(8,128)(2,1)} %all-gather.5.cloned.1.call-done.basis, bf16[7,2,1024,256]{3,2,1,0:T(8,128)(2,1)} %bitcast.4, bf16[2048,3584]{1,0:T(8,128)(2,1)} %weight.1), custom_call_target="tpu_custom_call" | custom-call | flops 15032385536 | bytes 44040192 | tf_op jit(solution)/shard_map/apply_update/pallas_call | solution.py:263
  252.0 0.0 copy-done.3
  252.0 0.0 copy-start.2
  252.0 0.0 copy-start.1
  252.0 1.9 copy.11
  253.9 1.5 copy-done.2
  255.3 1.8 copy.12
  257.2 0.0 copy-done.1
Async XLA Ops:
  7.2 1.6 copy-start
  7.2 42.4 %reduce-scatter.2.cloned.1.call-start = ((), (), s32[]{:S(2)}) async-start(), calls=%async_computation.1 | async-start | bytes 2359296 | tf_op jit(solution)/shard_map/reduce_scatter | solution.py:290
  14.1 65.2 %all-gather.3.cloned.1.call-start = ((), (), s32[]{:S(2)}) async-start(), calls=%async_computation.2 | async-start | bytes 2359296 | tf_op jit(solution)/shard_map/all_gather | solution.py:291
  49.6 180.3 %all-gather.5.cloned.1.call-start = ((), (), s32[]{:S(2)}) async-start(), calls=%async_computation.3 | async-start | bytes 18874368 | tf_op jit(solution)/shard_map/all_gather | solution.py:293
  229.9 22.1 %copy-start.3 = (f32[256,3584]{1,0:T(8,128)S(1)}, f32[256,3584]{1,0:T(8,128)}, u32[]{:S(2)}) copy-start(f32[256,3584]{1,0:T(8,128)} %get-tuple-element.17) | copy-start | bytes 11010052
  252.0 3.4 %copy-start.2 = (f32[256,3584]{1,0:T(8,128)S(1)}, f32[256,3584]{1,0:T(8,128)}, u32[]{:S(2)}) copy-start(f32[256,3584]{1,0:T(8,128)} %get-tuple-element.18) | copy-start | bytes 11010052
  252.0 5.2 %copy-start.1 = (bf16[1024,1024]{1,0:T(8,128)(2,1)S(1)}, bf16[1024,1024]{1,0:T(8,128)(2,1)}, u32[]{:S(2)}) copy-start(bf16[1024,1024]{1,0:T(8,128)(2,1)} %param.6) | copy-start | bytes 6291460
Sparse Core Ops, SparseCore 0:
  14.2 35.3 reduce-scatter.1
  51.2 28.0 all-gather.2
  80.9 148.9 all-gather.4

commit v2 on v1

--- a/solution.py
+++ b/solution.py
@@ -19,16 +19,29 @@
 
 
 def row_kernel(
-    A, B, steps, rb, W,
-    proj, hidden, first, second,
-    gathered, new_first, new_second,
+    A, B, Z, steps, rb, W, chunks,
+    part, hidden, first, second, basis,
+    gathered, new_first, new_second, spread,
+    cross, chip, terms, proj, bas,
     hid, par, one_b, one_a, mid_b, mid_a, two_b, two_a, gat, mom_one, mom_two,
     load, out_sem,
     s1b, r1b, s1a, r1a, s2b, r2b, s2a, r2a,
     sgb, rgb, sga, rga, srb, rrb, sra, rra,
+    scx, rcx, szr, rzr, szg, rzg, spg, rpg,
+    sbu, sbd, rbc, sbp, rbp, bas_in, bas_out,
 ):
     row = lax.axis_index("row")
     a, b = row // B, lax.rem(row, B)
+    col = lax.axis_index("col")
+    z, core = col // 2, lax.rem(col, 2)
+    partner = {"col": z * 2 + 1 - core}
+    pieces = sorted(
+        [(i, j) for i in range(A) for j in range(B)],
+        key=lambda d: -(d[0] > 0) - (d[1] > 0),
+    )
+
+    def to_z(k):
+        return {"col": lax.rem(z + k, Z) * 2 + core}
 
     def to_a(k):
         return {"row": lax.rem(a + k, A) * B + b}
@@ -58,13 +71,20 @@
             device_id=device, device_id_type=MESH,
         )
 
+    def first_hop(s, da, db):
+        i, j = lax.rem(a + da, A), lax.rem(b + db, B)
+        if db:
+            n = (db - 1) * A + da
+            yield remote(par.at[s, 0, i, j], one_b.at[s, db - 1, i],
+                         s1b.at[s, n], r1b.at[s, n], to_b(db))
+        if da:
+            n = (da - 1) * B + db
+            yield remote(par.at[s, 1, i, j], one_a.at[s, da - 1, j],
+                         s1a.at[s, n], r1a.at[s, n], to_a(da))
+
     def first_hops(s):
-        for k in range(1, B):
-            yield remote(par.at[s, 0, :, lax.rem(b + k, B)], one_b.at[s, k - 1],
-                         s1b.at[s, k - 1], r1b.at[s, k - 1], to_b(k))
-        for k in range(1, A):
-            yield remote(par.at[s, 1, lax.rem(a + k, A)], one_a.at[s, k - 1],
-                         s1a.at[s, k - 1], r1a.at[s, k - 1], to_a(k))
+        for piece in pieces:
+            yield from first_hop(s, *piece)
 
     def second_hops(s):
         for k in range(1, A):
@@ -94,11 +114,78 @@
                 i = (j - 1) * (B - 1) + k - 1
                 yield remote(block, block, sra.at[s, i], rra.at[s, i], to_b(k))
 
+    def block_of(p):
+        return lax.rem(a + pieces[p][0], A), lax.rem(b + pieces[p][1], B)
+
+    def crossing(p):
+        i, j = block_of(p)
+        yield remote(part.at[i, j, 1 - core], cross.at[p], scx.at[p], rcx.at[p], partner)
+
+    def scatters(p):
+        for k in range(1, Z):
+            yield remote(chip.at[p, lax.rem(z + k, Z)], terms.at[p, k - 1],
+                         szr.at[p, k - 1], rzr.at[p, k - 1], to_z(k))
+
+    def gathers(p):
+        i, j = block_of(p)
+        block = proj.at[i, j, core, z]
+        for k in range(1, Z):
+            yield remote(block, block, szg.at[p, k - 1], rzg.at[p, k - 1], to_z(k))
+
+    def shares(p, first_k, last_k):
+        i, j = block_of(p)
+        for k in range(first_k, last_k):
+            block = proj.at[i, j, core, lax.rem(z + k, Z)]
+            yield remote(block, block, spg.at[p, k], rpg.at[p, k], partner)
+
+    source = row
+    far = jnp.abs(z - source)
+
+    def upward(i):
+        block = bas.at[core, i]
+        return remote(block, block, sbu.at[i], rbc.at[i], {"col": lax.rem(z + 1, Z) * 2 + core})
+
+    def downward(i):
+        block = bas.at[core, i]
+        return remote(block, block, sbd.at[i], rbc.at[i], {"col": lax.rem(z + Z - 1, Z) * 2 + core})
+
+    def beside(i):
+        block = bas.at[core, i]
+        return remote(block, block, sbp.at[i], rbp.at[i], partner)
+
+    goes_up = (z >= source) & (z < Z - 1)
+    goes_down = (z <= source) & (z > 0)
+
+    def spread_step(it):
+        i = it - far
+
+        @pl.when((i >= 0) & (i < chunks))
+        def _():
+            @pl.when(far > 0)
+            def _():
+                upward(i).wait_recv()
+
+            @pl.when(goes_up)
+            def _():
+                upward(i).start()
+
+            @pl.when(goes_down)
+            def _():
+                downward(i).start()
+
+            beside(i).start()
+
     def result(s):
         return pltpu.make_async_copy(gat.at[s], gathered.at[s], out_sem.at[0, s])
 
     def every(body):
         lax.fori_loop(0, steps, lambda s, c: (body(s), c)[1], 0)
+
+    own_basis = pltpu.make_async_copy(basis, bas.at[core], bas_in)
+
+    @pl.when(far == 0)
+    def _():
+        own_basis.start()
 
     every(lambda s: [c.start() for c in loads(s)])
 
@@ -107,25 +194,72 @@
         pl.semaphore_signal(barrier, inc=1, device_id=to_b(k), device_id_type=MESH)
     for k in range(1, A):
         pl.semaphore_signal(barrier, inc=1, device_id=to_a(k), device_id_type=MESH)
-    pl.semaphore_wait(barrier, A + B - 2)
-
-    f32 = jnp.float32
+    for k in range(1, Z):
+        pl.semaphore_signal(barrier, inc=1, device_id=to_z(k), device_id_type=MESH)
+    pl.semaphore_signal(barrier, inc=1, device_id=partner, device_id_type=MESH)
+    pl.semaphore_wait(barrier, A + B + Z - 2)
+
+    f32, bf16 = jnp.float32, jnp.bfloat16
+    count = len(pieces)
+    for p in range(count):
+        for c in crossing(p):
+            c.start()
+    for it in range(count + 3):
+        p = it
+        if 0 <= p < count:
+            i, j = block_of(p)
+            for c in crossing(p):
+                c.wait_recv()
+            chip[p] = (part[i, j, core].astype(f32) + cross[p].astype(f32)).astype(bf16)
+            for c in scatters(p):
+                c.start()
+        p = it - 1
+        if 0 <= p < count:
+            i, j = block_of(p)
+            for c in scatters(p):
+                c.wait_recv()
+            total = chip[p, z].astype(f32)
+            for k in range(Z - 1):
+                total += terms[p, k].astype(f32)
+            proj[i, j, core, z] = total.astype(bf16)
+            for c in gathers(p):
+                c.start()
+            for c in shares(p, 0, 1):
+                c.start()
+        p = it - 2
+        if 0 <= p < count:
+            for c in gathers(p):
+                c.wait_recv()
+            for c in shares(p, 1, Z):
+                c.start()
+        p = it - 3
+        if 0 <= p < count:
+            i, j = block_of(p)
+            for c in shares(p, 0, Z):
+                c.wait_recv()
+
+            def partial_step(s, carry, p=p, i=i, j=j):
+                if p == 0:
+                    loads(s)[0].wait()
+                got = jnp.dot(proj[i, j].reshape(rb, -1), hid[s], preferred_element_type=f32)
+                par[s, 0, i, j] = got[:, :W].astype(bf16)
+                par[s, 1, i, j] = got[:, W:].astype(bf16)
+                for c in first_hop(s, *pieces[p]):
+                    c.start()
+                return carry
+
+            lax.fori_loop(0, steps, partial_step, 0)
+
+    @pl.when(far == 0)
+    def _():
+        own_basis.wait()
 
     def turn(it, carry):
+        spread_step(it)
+
         @pl.when(it < steps)
         def _():
             s = it
-            loads(s)[0].wait()
-            for t in range(2):
-                got = jnp.dot(proj[...], hid[s, :, t * W:(t + 1) * W],
-                              preferred_element_type=f32)
-                par[s, t] = got.astype(jnp.bfloat16).reshape(A, B, rb, W)
-            for c in first_hops(s):
-                c.start()
-
-        @pl.when((it >= 1) & (it < steps + 1))
-        def _():
-            s = it - 1
             for c in first_hops(s):
                 c.wait_recv()
             for i in range(A):
@@ -141,9 +275,9 @@
             for c in second_hops(s):
                 c.start()
 
-        @pl.when((it >= 2) & (it < steps + 2))
-        def _():
-            s = it - 2
+        @pl.when((it >= 1) & (it < steps + 1))
+        def _():
+            s = it - 1
             for c in second_hops(s):
                 c.wait_recv()
             for c in loads(s)[1:]:
@@ -170,24 +304,45 @@
             for c in stores(s):
                 c.start()
 
+        @pl.when((it >= 2) & (it < steps + 2))
+        def _():
+            s = it - 2
+            for c in own_sends(s):
+                c.wait_recv()
+            for c in relays(s):
+                c.start()
+
         @pl.when((it >= 3) & (it < steps + 3))
         def _():
             s = it - 3
-            for c in own_sends(s):
-                c.wait_recv()
             for c in relays(s):
-                c.start()
-
-        @pl.when(it >= 4)
-        def _():
-            s = it - 4
-            for c in relays(s):
                 c.wait_recv()
             result(s).start()
 
         return carry
 
-    lax.fori_loop(0, steps + 4, turn, 0)
+    lax.fori_loop(0, max(steps + 3, chunks + Z - 1), turn, 0)
+
+    def finish_basis(i, carry):
+        beside(i).wait()
+
+        @pl.when(goes_up)
+        def _():
+            upward(i).wait_send()
+
+        @pl.when(goes_down)
+        def _():
+            downward(i).wait_send()
+
+        return carry
+
+    lax.fori_loop(0, chunks, finish_basis, 0)
+    spread_out = pltpu.make_async_copy(bas, spread, bas_out)
+    spread_out.start()
+    for p in range(count):
+        for group in (crossing(p), scatters(p), gathers(p), shares(p, 0, Z)):
+            for c in group:
+                c.wait_send()
 
     def finish(s):
         for group in (first_hops, second_hops, own_sends, relays):
@@ -198,13 +353,21 @@
         result(s).wait()
 
     every(finish)
-
-
-def row_part(rows, proj, hidden, first, second):
+    spread_out.wait()
+
+
+def row_part(rows, banks, part, hidden, first, second, basis):
+    Z = banks // 2
     B = 2 if rows % 2 == 0 else 1
     A = rows // B
-    rank, tokens = proj.shape
+    rank, tokens = part.shape
     rb, cols = first.shape
+    rk = rb // banks
+    count = rows
+    chunks = 8
+    depth = basis.shape[0] // chunks
+    part = part.reshape(A, B, 2, Z, rk, tokens)
+    basis = basis.reshape(chunks, depth, rank)
     W = 256 if cols % 512 == 0 else 128
     steps = cols // (2 * W)
     bf16, f32 = jnp.bfloat16, jnp.float32
@@ -214,18 +377,29 @@
     def pair(n):
         return [pltpu.SemaphoreType.DMA((steps, n)), pltpu.SemaphoreType.DMA((steps, n))]
 
+    def two(*shape):
+        return [pltpu.SemaphoreType.DMA(shape), pltpu.SemaphoreType.DMA(shape)]
+
+    one = pltpu.SemaphoreType.DMA((chunks,))
+
     anywhere = pl.BlockSpec(memory_space=pl.ANY)
     return pl.pallas_call(
-        functools.partial(row_kernel, A, B, steps, rb, W),
+        functools.partial(row_kernel, A, B, Z, steps, rb, W, chunks),
         name="row_part",
         out_shape=(
             jax.ShapeDtypeStruct((steps, 2, A, B, rb, W), bf16),
             jax.ShapeDtypeStruct(first.shape, f32),
             jax.ShapeDtypeStruct(second.shape, f32),
+            jax.ShapeDtypeStruct((2,) + basis.shape, bf16),
         ),
-        in_specs=[pl.BlockSpec(memory_space=pltpu.VMEM), anywhere, anywhere, anywhere],
-        out_specs=(anywhere, anywhere, anywhere),
+        in_specs=[pl.BlockSpec(memory_space=pltpu.VMEM)] + [anywhere] * 4,
+        out_specs=(anywhere,) * 4,
         scratch_shapes=[
+            pltpu.VMEM((count, Z, rk, tokens), bf16),
+            pltpu.VMEM((count, Z, rk, tokens), bf16),
+            pltpu.VMEM((count, Z - 1, rk, tokens), bf16),
+            pltpu.VMEM((A, B, 2, Z, rk, tokens), bf16),
+            pltpu.VMEM((2,) + basis.shape, bf16),
             pltpu.VMEM((steps, tokens, 2 * W), bf16),
             pltpu.VMEM((steps, 2, A, B, rb, W), bf16),
             pltpu.VMEM((steps, nb, A, rb, W), bf16),
@@ -239,63 +413,59 @@
             pltpu.VMEM((steps, rb, 2 * W), f32),
             pltpu.SemaphoreType.DMA((3, steps)),
             pltpu.SemaphoreType.DMA((3, steps)),
-        ] + pair(nb) + pair(na) + pair(na) + pair(nb) + pair(nb) + pair(na) + pair(nr) + pair(nr),
+        ] + pair(nb * A) + pair(na * B) + pair(na) + pair(nb) + pair(nb) + pair(na) + pair(nr) + pair(nr)
+        + two(count) + two(count, Z - 1) + two(count, Z - 1) + two(count, Z)
+        + [one] * 5 + [pltpu.SemaphoreType.DMA, pltpu.SemaphoreType.DMA],
         compiler_params=pltpu.CompilerParams(
             collective_id=0, has_side_effects=True, vmem_limit_bytes=60 << 20
         ),
         cost_estimate=pl.CostEstimate(
             flops=2 * rank * tokens * cols * 8, bytes_accessed=400 << 20, transcendentals=0
         ),
-    )(proj, hidden, first, second)
-
-
-def update_kernel(W, which, basis, direction, weight, out):
+    )(part, hidden, first, second, basis)
+
+
+def update_kernel(W, basis, direction, weight, out):
     for t in range(2):
         cols = slice(t * W, (t + 1) * W)
         update = jnp.dot(basis[...], direction[0, t], preferred_element_type=jnp.float32)
         out[:, cols] = (weight[:, cols].astype(jnp.float32) - step_size * update).astype(jnp.bfloat16)
 
 
-def apply_update(index, basis, gathered, weight):
+def apply_update(basis, gathered, weight):
     steps, _, rank, W = gathered.shape
     rows, cols = weight.shape
-    wide = pl.BlockSpec((rows, 2 * W), lambda j, r: (0, j))
+    wide = pl.BlockSpec((rows, 2 * W), lambda j: (0, j))
     return pl.pallas_call(
         functools.partial(update_kernel, W),
         name="apply_update",
         out_shape=jax.ShapeDtypeStruct(weight.shape, weight.dtype),
-        grid_spec=pltpu.PrefetchScalarGridSpec(
-            num_scalar_prefetch=1,
-            grid=(steps,),
-            in_specs=[
-                pl.BlockSpec((rows, rank), lambda j, r: (r[0], 0), pipeline_mode=pl.Buffered(1)),
-                pl.BlockSpec((1, 2, rank, W), lambda j, r: (j, 0, 0, 0)),
-                wide,
-            ],
-            out_specs=wide,
-        ),
+        grid=(steps,),
+        in_specs=[
+            pl.BlockSpec((rows, rank), lambda j: (0, 0), pipeline_mode=pl.Buffered(1)),
+            pl.BlockSpec((1, 2, rank, W), lambda j: (j, 0, 0, 0)),
+            wide,
+        ],
+        out_specs=wide,
         compiler_params=pltpu.CompilerParams(
             dimension_semantics=("arbitrary",), vmem_limit_bytes=56 << 20
         ),
         cost_estimate=pl.CostEstimate(
             flops=2 * rank * rows * cols, bytes_accessed=3 * weight.size * 2, transcendentals=0
         ),
-    )(index, basis, gathered, weight)
-
-
-def local(rows, out_grad, hidden, basis, weight, first_moment, second_moment):
+    )(basis, gathered, weight)
+
+
+def local(rows, banks, out_grad, hidden, basis, weight, first_moment, second_moment):
     part = lax.dot_general(
         basis, out_grad, (((0,), (1,)), ((), ())), preferred_element_type=jnp.float32
     ).astype(jnp.bfloat16)
-    proj = lax.psum_scatter(part, "col", scatter_dimension=0, tiled=True)
-    proj = lax.all_gather(proj, "col", axis=0, tiled=True)
-    late, proj = lax.optimization_barrier((basis, proj))
-    whole = lax.all_gather(late, "col", axis=0, tiled=True)
-    gathered, new_first, new_second = row_part(rows, proj, hidden, first_moment, second_moment)
+    gathered, new_first, new_second, spread = row_part(
+        rows, banks, part, hidden, first_moment, second_moment, basis
+    )
     steps, W = gathered.shape[0], gathered.shape[-1]
     gathered = gathered.reshape(steps, 2, -1, W)
-    index = lax.axis_index("row").astype(jnp.int32).reshape(1)
-    new_weight = apply_update(index, whole, gathered, weight)
+    new_weight = apply_update(spread.reshape(-1, basis.shape[1]), gathered, weight)
     return (new_weight, new_first, new_second)
 
 
@@ -310,6 +480,6 @@
     )
     out_specs = (P("row", "col"), P("row", "col"), P("row", "col"))
     return jax.shard_map(
-        functools.partial(local, mesh.shape["row"]),
+        functools.partial(local, mesh.shape["row"], mesh.shape["col"]),
         mesh=mesh, in_specs=in_specs, out_specs=out_specs, check_vma=False,
     )

time: 268 us -> 206 us (0.77); the launches traced: 264 us -> 206 us
  waiting for transfers between devices: 89.4 us -> 0 us
  Pallas kernels: 148 us -> 193 us
  between operations: 13.8 us -> 0.66 us
    all_gather x2 -> x0, waiting for transfers between devices: 53.9 us -> none  [the longest x1 29.6 us: local(): proj = lax.all_gather(proj, 'col', axis=0, tiled=True)]
    pallas_call x1, Pallas kernels: 126 us -> 171 us  [row_part(): pl.pallas_call(functools.partial(row_kernel, A, B, Z, steps, rb, W, chunk...]
    reduce_scatter x1 -> x0, waiting for transfers between devices: 35.5 us -> none  [local(): proj = lax.psum_scatter(part, 'col', scatter_dimension=0, tiled=True)]
  transfers between devices with their start and end apart: 3 -> 0, of which waited for: 3 -> 0; matrix products, arithmetic and copies ran while one was open for 0% -> 0% of each run, Pallas kernels for 48% -> 0%
where the time goes in v2:
time: 206 us
  Pallas kernels  193 us (94%)
  local copies, waits for them, and re-layouts  6.79 us (3%)
  matrix products  5.29 us (3%)
    pallas_call x1, Pallas kernels, row_part(): pl.pallas_call(functools.partial(row_kernel, A, B, Z, steps, rb, W, chunk...  171 us
    pallas_call x1, Pallas kernels, apply_update(): pl.pallas_call(functools.partial(update_kernel, W), name='apply_update',...  22.4 us
    unnamed x10, local copies, waits for them, and re-layouts  6.79 us
    dot_general x1, matrix products, local(): lax.dot_general(basis, out_grad, (((0,), (1,)), ((), ())), preferred_elem...  5.29 us

profile of v2, /device:TPU:25, one launch (start us, length us, event | category | flops | bytes accessed | tf_op | source)
XLA Modules:
  0.0 205.8 jit_solution(6515898445704096991)
XLA Ops:
  0.6 0.0 copy-start
  0.6 1.6 copy-done
  2.2 5.3 %convolution_convert_fusion = bf16[1024,1024]{1,0:T(8,128)(2,1)} fusion(bf16[1024,1024]{1,0:T(8,128)(2,1)} %param.8, bf16[1024,1024]{1,0:T(8,128)(2,1)S(1)} %copy-done), kind=kOutput, calls=%fused_computation | convolution fusion | flops 2148532224 | bytes 6291456 | tf_op jit(solution)/shard_map/dot_general | solution.py:460
  7.5 170.6 %row_part.1 = (bf16[7,2,2,2,256,256]{5,4,3,2,1,0:T(8,128)(2,1)}, f32[256,3584]{1,0:T(8,128)}, f32[256,3584]{1,0:T(8,128)}, bf16[2,8,128,1024]{3,2,1,0:T(8,128)(2,1)}) custom-call(bf16[2,2,2,4,32,1024]{5,4,3,2,1,0:T(8,128)(2,1)} %bitcast.9, bf16[1024,3584]{1,0:T(8,128)(2,1)} %hidden.1, f32[256,3584]{1,0:T(8,128)} %first.1, f32[256,3584]{1,0:T(8,128)} %second.1, ...), custom_call_target="tpu_custom_call" | custom-call | flops 60129542144 | bytes 419430400 | tf_op jit(solution)/shard_map/row_part/pallas_call | solution.py:386
  178.1 0.0 copy-start.3
  178.2 22.4 %apply_update.1 = bf16[2048,3584]{1,0:T(8,128)(2,1)} custom-call(bf16[2048,1024]{1,0:T(8,128)(2,1)} %bitcast.8, bf16[7,2,1024,256]{3,2,1,0:T(8,128)(2,1)} %bitcast.7, bf16[2048,3584]{1,0:T(8,128)(2,1)} %weight.1), custom_call_target="tpu_custom_call" | custom-call | flops 15032385536 | bytes 44040192 | tf_op jit(solution)/shard_map/apply_update/pallas_call | solution.py:439
  200.6 0.0 copy-done.3
  200.6 0.0 copy-start.2
  200.6 0.0 copy-start.1
  200.6 1.9 copy.11
  202.5 1.5 copy-done.2
  203.9 1.8 copy.12
  205.8 0.0 copy-done.1
Async XLA Ops:
  0.6 1.6 copy-start
  178.1 22.4 %copy-start.3 = (f32[256,3584]{1,0:T(8,128)S(1)}, f32[256,3584]{1,0:T(8,128)}, u32[]{:S(2)}) copy-start(f32[256,3584]{1,0:T(8,128)} %get-tuple-element.15) | copy-start | bytes 11010052
  200.6 3.4 %copy-start.2 = (f32[256,3584]{1,0:T(8,128)S(1)}, f32[256,3584]{1,0:T(8,128)}, u32[]{:S(2)}) copy-start(f32[256,3584]{1,0:T(8,128)} %get-tuple-element.16) | copy-start | bytes 11010052
  200.6 5.2 %copy-start.1 = (bf16[1024,1024]{1,0:T(8,128)(2,1)S(1)}, bf16[1024,1024]{1,0:T(8,128)(2,1)}, u32[]{:S(2)}) copy-start(bf16[1024,1024]{1,0:T(8,128)(2,1)} %param.6) | copy-start | bytes 6291460

commit v3 on v2

--- a/solution.py
+++ b/solution.py
@@ -204,51 +204,48 @@
     for p in range(count):
         for c in crossing(p):
             c.start()
-    for it in range(count + 3):
-        p = it
-        if 0 <= p < count:
-            i, j = block_of(p)
-            for c in crossing(p):
-                c.wait_recv()
-            chip[p] = (part[i, j, core].astype(f32) + cross[p].astype(f32)).astype(bf16)
-            for c in scatters(p):
+
+    def scatter(p):
+        i, j = block_of(p)
+        for c in crossing(p):
+            c.wait_recv()
+        chip[p] = (part[i, j, core].astype(f32) + cross[p].astype(f32)).astype(bf16)
+        for c in scatters(p):
+            c.start()
+
+    scatter(0)
+    for p in range(count):
+        i, j = block_of(p)
+        for c in scatters(p):
+            c.wait_recv()
+        total = chip[p, z].astype(f32)
+        for k in range(Z - 1):
+            total += terms[p, k].astype(f32)
+        proj[i, j, core, z] = total.astype(bf16)
+        for c in gathers(p):
+            c.start()
+        for c in shares(p, 0, 1):
+            c.start()
+        if p + 1 < count:
+            scatter(p + 1)
+        for c in gathers(p):
+            c.wait_recv()
+        for c in shares(p, 1, Z):
+            c.start()
+        for c in shares(p, 0, Z):
+            c.wait_recv()
+
+        def partial_step(s, carry, p=p, i=i, j=j):
+            if p == 0:
+                loads(s)[0].wait()
+            got = jnp.dot(proj[i, j].reshape(rb, -1), hid[s], preferred_element_type=f32)
+            par[s, 0, i, j] = got[:, :W].astype(bf16)
+            par[s, 1, i, j] = got[:, W:].astype(bf16)
+            for c in first_hop(s, *pieces[p]):
                 c.start()
-        p = it - 1
-        if 0 <= p < count:
-            i, j = block_of(p)
-            for c in scatters(p):
-                c.wait_recv()
-            total = chip[p, z].astype(f32)
-            for k in range(Z - 1):
-                total += terms[p, k].astype(f32)
-            proj[i, j, core, z] = total.astype(bf16)
-            for c in gathers(p):
-                c.start()
-            for c in shares(p, 0, 1):
-                c.start()
-        p = it - 2
-        if 0 <= p < count:
-            for c in gathers(p):
-                c.wait_recv()
-            for c in shares(p, 1, Z):
-                c.start()
-        p = it - 3
-        if 0 <= p < count:
-            i, j = block_of(p)
-            for c in shares(p, 0, Z):
-                c.wait_recv()
-
-            def partial_step(s, carry, p=p, i=i, j=j):
-                if p == 0:
-                    loads(s)[0].wait()
-                got = jnp.dot(proj[i, j].reshape(rb, -1), hid[s], preferred_element_type=f32)
-                par[s, 0, i, j] = got[:, :W].astype(bf16)
-                par[s, 1, i, j] = got[:, W:].astype(bf16)
-                for c in first_hop(s, *pieces[p]):
-                    c.start()
-                return carry
-
-            lax.fori_loop(0, steps, partial_step, 0)
+            return carry
+
+        lax.fori_loop(0, steps, partial_step, 0)
 
     @pl.when(far == 0)
     def _():
@@ -425,35 +422,38 @@
     )(part, hidden, first, second, basis)
 
 
-def update_kernel(W, basis, direction, weight, out):
+def update_kernel(W, basis, direction, weight, first, second, out, first_out, second_out):
+    first_out[...] = first[...]
+    second_out[...] = second[...]
     for t in range(2):
         cols = slice(t * W, (t + 1) * W)
         update = jnp.dot(basis[...], direction[0, t], preferred_element_type=jnp.float32)
         out[:, cols] = (weight[:, cols].astype(jnp.float32) - step_size * update).astype(jnp.bfloat16)
 
 
-def apply_update(basis, gathered, weight):
+def apply_update(basis, gathered, weight, first, second):
     steps, _, rank, W = gathered.shape
     rows, cols = weight.shape
     wide = pl.BlockSpec((rows, 2 * W), lambda j: (0, j))
+    moment = pl.BlockSpec((first.shape[0], 2 * W), lambda j: (0, j))
     return pl.pallas_call(
         functools.partial(update_kernel, W),
         name="apply_update",
-        out_shape=jax.ShapeDtypeStruct(weight.shape, weight.dtype),
+        out_shape=tuple(jax.ShapeDtypeStruct(x.shape, x.dtype) for x in (weight, first, second)),
         grid=(steps,),
         in_specs=[
             pl.BlockSpec((rows, rank), lambda j: (0, 0), pipeline_mode=pl.Buffered(1)),
             pl.BlockSpec((1, 2, rank, W), lambda j: (j, 0, 0, 0)),
-            wide,
+            wide, moment, moment,
         ],
-        out_specs=wide,
+        out_specs=(wide, moment, moment),
         compiler_params=pltpu.CompilerParams(
             dimension_semantics=("arbitrary",), vmem_limit_bytes=56 << 20
         ),
         cost_estimate=pl.CostEstimate(
             flops=2 * rank * rows * cols, bytes_accessed=3 * weight.size * 2, transcendentals=0
         ),
-    )(basis, gathered, weight)
+    )(basis, gathered, weight, first, second)
 
 
 def local(rows, banks, out_grad, hidden, basis, weight, first_moment, second_moment):
@@ -465,8 +465,9 @@
     )
     steps, W = gathered.shape[0], gathered.shape[-1]
     gathered = gathered.reshape(steps, 2, -1, W)
-    new_weight = apply_update(spread.reshape(-1, basis.shape[1]), gathered, weight)
-    return (new_weight, new_first, new_second)
+    return apply_update(
+        spread.reshape(-1, basis.shape[1]), gathered, weight, new_first, new_second
+    )
 
 
 def solution(mesh):

time: 206 us -> 195 us (0.947)
  Pallas kernels: 193 us -> 186 us
  local copies, waits for them, and re-layouts: 6.79 us -> 1.6 us
    pallas_call x1, Pallas kernels: 171 us -> 160 us  [row_part(): pl.pallas_call(functools.partial(row_kernel, A, B, Z, steps, rb, W, chunk...]
    unnamed x10 -> x4, local copies, waits for them, and re-layouts: 6.79 us -> 1.6 us
    pallas_call x1, Pallas kernels: 22.4 us -> 25.6 us  [apply_update(): pl.pallas_call(functools.partial(update_kernel, W), name='apply_update',...]
where the time goes in v3:
time: 195 us; the launch traced here: 193 us
  Pallas kernels  186 us (95%)
  matrix products  5.29 us (3%)
    pallas_call x1, Pallas kernels, row_part(): pl.pallas_call(functools.partial(row_kernel, A, B, Z, steps, rb, W, chunk...  160 us
    pallas_call x1, Pallas kernels, apply_update(): pl.pallas_call(functools.partial(update_kernel, W), name='apply_update',...  25.6 us
    dot_general x1, matrix products, local(): lax.dot_general(basis, out_grad, (((0,), (1,)), ((), ())), preferred_elem...  5.29 us

profile of v3, /device:TPU:25, one launch (start us, length us, event | category | flops | bytes accessed | tf_op | source)
XLA Modules:
  0.0 193.4 jit_solution(17638550819727840459)
XLA Ops:
  0.6 0.0 copy-start
  0.6 1.6 copy-done
  2.2 5.3 %convolution_convert_fusion = bf16[1024,1024]{1,0:T(8,128)(2,1)} fusion(bf16[1024,1024]{1,0:T(8,128)(2,1)} %param.8, bf16[1024,1024]{1,0:T(8,128)(2,1)S(1)} %copy-done), kind=kOutput, calls=%fused_computation | convolution fusion | flops 2148532224 | bytes 6291456 | tf_op jit(solution)/shard_map/dot_general | solution.py:460
  7.5 160.3 %row_part.1 = (bf16[7,2,2,2,256,256]{5,4,3,2,1,0:T(8,128)(2,1)}, f32[256,3584]{1,0:T(8,128)}, f32[256,3584]{1,0:T(8,128)}, bf16[2,8,128,1024]{3,2,1,0:T(8,128)(2,1)}) custom-call(bf16[2,2,2,4,32,1024]{5,4,3,2,1,0:T(8,128)(2,1)} %bitcast.9, bf16[1024,3584]{1,0:T(8,128)(2,1)} %hidden.1, f32[256,3584]{1,0:T(8,128)} %first.1, f32[256,3584]{1,0:T(8,128)} %second.1, ...), custom_call_target="tpu_custom_call" | custom-call | flops 60129542144 | bytes 419430400 | tf_op jit(solution)/shard_map/row_part/pallas_call | solution.py:383
  167.8 0.0 copy-start.1
  167.8 25.6 %apply_update.1 = (bf16[2048,3584]{1,0:T(8,128)(2,1)}, f32[256,3584]{1,0:T(8,128)}, f32[256,3584]{1,0:T(8,128)}) custom-call(bf16[2048,1024]{1,0:T(8,128)(2,1)} %bitcast.8, bf16[7,2,1024,256]{3,2,1,0:T(8,128)(2,1)} %bitcast.7, bf16[2048,3584]{1,0:T(8,128)(2,1)} %weight.1, f32[256,3584]{1,0:T(8,128)} %get-tuple-element.9.first, ...), custom_call_target="tpu_custom_call" | custom-call | flops 15032385536 | bytes 44040192 | tf_op jit(solution)/shard_map/apply_update/pallas_call | solution.py:439
  193.4 0.0 copy-done.1
Async XLA Ops:
  0.6 1.6 copy-start
  167.8 25.6 %copy-start.1 = (bf16[1024,1024]{1,0:T(8,128)(2,1)S(1)}, bf16[1024,1024]{1,0:T(8,128)(2,1)}, u32[]{:S(2)}) copy-start(bf16[1024,1024]{1,0:T(8,128)(2,1)} %param.6) | copy-start | bytes 6291460
